TPU v7x, 32 devices: a whole 2x2x4 slice. The times are simulated.
32 devices in a mesh: gx: 8 (over z, x), gy: 2 (over y), gz: 2 (over core).
Axes of the slice: x: 2, y: 2, z: 4, core: 2. Of those that a mesh axis runs over, the one named last changes fastest.
Arguments:
- velocity: float32 [3, 128, 64, 256], P(None, 'gx', 'gy', 'gz'), may hold values from -6 to 6
- conv_prev: float32 [3, 128, 64, 256], P(None, 'gx', 'gy', 'gz'), may hold values from -8 to 8
Outputs:
- convection: float32 [3, 128, 64, 256], P(None, 'gx', 'gy', 'gz')
- updated: float32 [3, 128, 64, 256], P(None, 'gx', 'gy', 'gz')
All inputs are finite; a program needn't handle non-finite values.
Results may differ from a plain program's by a relative error of at most 0.00011.
Values sent between devices are 32-bit elements; how exact they have to be, the bound alone decides.
A program may use at most 64 MiB of HBM per device.

v0:
```python
import jax
import jax.numpy as jnp
from jax import lax
from jax.sharding import PartitionSpec as P

time_step = 1.0
gamma_now = 5.0 / 12.0
zeta_old = -17.0 / 60.0
viscosity = 0.1
compact_pairs = ((1.0 / 3.0, 1.0), (2.0 / 11.0, 1.0))


def entering(part, axis, combine, identity, reverse):
    count = lax.axis_size(axis)
    place = lax.axis_index(axis)
    ahead = count - 1 - place if reverse else place
    gathered = jax.tree.map(lambda a: lax.all_gather(a, axis), part)
    state = jax.tree.map(lambda a, e: jnp.zeros_like(a) + jnp.asarray(e, a.dtype), part, identity)

    def one(hop, state):
        source = count - 1 - hop if reverse else hop
        return combine(
            state, jax.tree.map(lambda a: lax.dynamic_index_in_dim(a, source, 0, False), gathered)
        )

    return lax.fori_loop(0, ahead, one, state)


def padded_2(block, sides, width):
    for axis, dim in sides:
        count = lax.axis_size(axis)
        forward = [(i, i + 1) for i in range(count - 1)]
        forward.append((count - 1, 0))
        backward = [(target, source) for source, target in forward]
        low = lax.ppermute(
            lax.slice_in_dim(block, block.shape[dim] - width, None, axis=dim), axis, forward
        )
        high = lax.ppermute(lax.slice_in_dim(block, 0, width, axis=dim), axis, backward)
        block = jnp.concatenate([low, block, high], axis=dim)
    return block


def line_table(off_value, center, total):
    coupling = jnp.float32(off_value)
    middle = jnp.float32(center)
    reach = 2.0 * jnp.abs(coupling)
    spread = jnp.sqrt((middle - reach) * (middle + reach))
    larger = 0.5 * (middle + spread)
    log_ratio = jnp.log1p(-spread / larger)
    steps = jnp.arange(1, total + 1).astype(jnp.float32)
    ratios = coupling / larger * jnp.expm1(steps * log_ratio) / jnp.expm1((steps + 1.0) * log_ratio)
    previous = jnp.concatenate([jnp.zeros((1,), jnp.float32), ratios[:-1]])
    pivots = middle - coupling * previous
    return (ratios, pivots)


def block_tables(off_value, center, total, start, length):
    ratios, pivots = line_table(off_value, center, total)
    ratio = lax.dynamic_slice_in_dim(ratios, start, length)
    pivot = lax.dynamic_slice_in_dim(pivots, start, length)
    unit = jnp.eye(length, dtype=jnp.float32)

    def forward_row(carry, items):
        ratio_now, pivot_now, unit_row = items
        fresh = unit_row / pivot_now - ratio_now * carry
        return (fresh, fresh)

    _, forward_matrix = lax.scan(
        forward_row, jnp.zeros((length,), jnp.float32), (ratio, pivot, unit)
    )

    def backward_row(carry, items):
        ratio_now, unit_row = items
        fresh = unit_row - ratio_now * carry
        return (fresh, fresh)

    _, backward_matrix = lax.scan(
        backward_row, jnp.zeros((length,), jnp.float32), (ratio, unit), reverse=True
    )
    left_gain = jnp.cumprod(-ratio)
    right_gain = jnp.cumprod(-ratio[::-1])[::-1]
    return (ratios, forward_matrix, backward_matrix, left_gain, right_gain)


def system_tables(couplings, total, start, length):
    pieces = [
        block_tables(off_value, center, total, start, length) for off_value, center in couplings
    ]
    return tuple((jnp.stack([piece[slot] for piece in pieces]) for slot in range(5)))


def along(vector, row_dim, rank):
    shape = [1] * rank
    shape[0] = vector.shape[0]
    shape[row_dim] = vector.shape[1]
    return vector.reshape(shape)


def compose(earlier, later):
    return (later[0] * earlier[0], later[0] * earlier[1] + later[1])


def solve_sweep(data, tables, pattern, row_dim, forward_move, backward_move):
    ratios, forward_matrix, backward_matrix, left_gain, right_gain = tables
    systems, length = left_gain.shape
    rank = data.ndim
    factor_shape = (systems,) + (1,) * (rank - 2)
    local_part = jnp.einsum(pattern, forward_matrix, data, precision=lax.Precision.HIGHEST)
    tail = lax.index_in_dim(local_part, length - 1, row_dim, keepdims=False)
    carry = forward_move((left_gain[:, length - 1].reshape(factor_shape), tail))[1]
    reduced = local_part + along(left_gain, row_dim, rank) * jnp.expand_dims(carry, row_dim)
    solved = jnp.einsum(pattern, backward_matrix, reduced, precision=lax.Precision.HIGHEST)
    head = lax.index_in_dim(solved, 0, row_dim, keepdims=False)
    after = backward_move((right_gain[:, 0].reshape(factor_shape), head))[1]
    return solved + along(right_gain, row_dim, rank) * jnp.expand_dims(after, row_dim)


def solve_reduced(data, tables, pattern, row_dim, place, count, gather_move):
    ratios, forward_matrix, backward_matrix, left_gain, right_gain = tables
    systems, length = left_gain.shape
    rank = data.ndim
    local_part = jnp.einsum(pattern, forward_matrix, data, precision=lax.Precision.HIGHEST)
    tail = lax.index_in_dim(local_part, length - 1, row_dim, keepdims=False)
    solved = jnp.einsum(pattern, backward_matrix, local_part, precision=lax.Precision.HIGHEST)
    head = lax.index_in_dim(solved, 0, row_dim, keepdims=False)
    tails, heads = gather_move((tail[None], head[None]))
    products = jnp.cumprod(-ratios.reshape(systems, count, length), axis=2)
    through = products[:, :, length - 1]
    before = jnp.concatenate(
        [jnp.ones((systems, count, 1), jnp.float32), products[:, :, : length - 1]], axis=2
    )
    coupling = jnp.sum(before * products, axis=2)
    unit = jnp.eye(count, dtype=jnp.float32)

    def weight_row(carry, items):
        factor, basis = items
        fresh = factor[:, None] * carry + basis[None, :]
        return (fresh, carry)

    _, ahead = lax.scan(weight_row, jnp.zeros((systems, count), jnp.float32), (through.T, unit))
    _, behind = lax.scan(
        weight_row, jnp.zeros((systems, count), jnp.float32), (through.T, unit), reverse=True
    )
    entries = jnp.einsum("psk,ks...->ps...", ahead, tails, precision=lax.Precision.HIGHEST)
    own_entry = entries[place]
    sources = heads + coupling.T.reshape((count, systems) + (1,) * (rank - 2)) * entries
    own_after = jnp.einsum(
        "sk,ks...->s...", behind[place], sources, precision=lax.Precision.HIGHEST
    )
    mixed_gain = jnp.einsum(
        "sik,sk->si", backward_matrix, left_gain, precision=lax.Precision.HIGHEST
    )
    return (
        solved
        + along(mixed_gain, row_dim, rank) * jnp.expand_dims(own_entry, row_dim)
        + along(right_gain, row_dim, rank) * jnp.expand_dims(own_after, row_dim)
    )


def outer_forward(pair):
    return entering(
        (pair[0], pair[1]), "gx", compose, (jnp.ones_like(pair[0]), jnp.zeros_like(pair[1])), False
    )


def outer_backward(pair):
    return entering(
        (pair[0], pair[1]), "gx", compose, (jnp.ones_like(pair[0]), jnp.zeros_like(pair[1])), True
    )


def normal_collect(pair):
    return (
        lax.all_gather(pair[0], "gy", axis=0, tiled=True),
        lax.all_gather(pair[1], "gy", axis=0, tiled=True),
    )


def wall_collect(pair):
    return (
        lax.all_gather(pair[0], "gy", axis=0, tiled=True),
        lax.all_gather(pair[1], "gy", axis=0, tiled=True),
    )


def compact_sides(shifted, centre):
    first = 7.0 / 9.0 * (shifted(1) - shifted(-1)) + 1.0 / 36.0 * (shifted(2) - shifted(-2))
    second = 12.0 / 11.0 * (shifted(1) - 2.0 * centre + shifted(-1)) + 3.0 / 44.0 * (
        shifted(2) - 2.0 * centre + shifted(-2)
    )
    return jnp.stack([first, second])


def body(velocity, conv_prev):
    components, rows_x, rows_y, rows_z = velocity.shape
    count_x = lax.axis_size("gx")
    count_y = lax.axis_size("gy")
    place_x = lax.axis_index("gx")
    place_y = lax.axis_index("gy")
    padded = padded_2(velocity, (("gx", 1), ("gy", 2), ("gz", 3)), 3)
    grid_x = jnp.arange(rows_x + 6)
    grid_y = jnp.arange(rows_y + 6)
    keep_x = ((grid_x >= 3) | (place_x > 0)) & ((grid_x < rows_x + 3) | (place_x < count_x - 1))
    keep_y = ((grid_y >= 3) | (place_y > 0)) & ((grid_y < rows_y + 3) | (place_y < count_y - 1))
    padded = jnp.where(keep_x[None, :, None, None] & keep_y[None, None, :, None], padded, 0.0)

    def cut(shift_x, shift_y, shift_z):
        return padded[
            :,
            3 + shift_x : 3 + shift_x + rows_x,
            3 + shift_y : 3 + shift_y + rows_y,
            3 + shift_z : 3 + shift_z + rows_z,
        ]

    def along_first(shift):
        return cut(shift, 0, 0)

    def along_second(shift):
        return cut(0, shift, 0)

    def along_third(shift):
        return cut(0, 0, shift)

    centre = cut(0, 0, 0)
    terms_x = compact_sides(along_first, centre)
    terms_y = compact_sides(along_second, centre)
    tables_x = system_tables(compact_pairs, rows_x * count_x, place_x * rows_x, rows_x)
    derived_x = solve_sweep(terms_x, tables_x, "sik,sckyz->sciyz", 2, outer_forward, outer_backward)
    tables_y = system_tables(compact_pairs, rows_y * count_y, place_y * rows_y, rows_y)
    derived_y = solve_reduced(
        terms_y, tables_y, "sik,scxkz->scxiz", 3, place_y, count_y, normal_collect
    )
    first_z = (
        45.0 * (along_third(1) - along_third(-1))
        - 9.0 * (along_third(2) - along_third(-2))
        + (along_third(3) - along_third(-3))
    ) / 60.0
    second_z = (
        2.0 * (along_third(3) + along_third(-3))
        - 27.0 * (along_third(2) + along_third(-2))
        + 270.0 * (along_third(1) + along_third(-1))
        - 490.0 * centre
    ) / 180.0
    convection = (
        velocity[0:1] * derived_x[0] + velocity[1:2] * derived_y[0] + velocity[2:3] * first_z
    )
    explicit = (
        velocity
        - time_step * (gamma_now * convection + zeta_old * conv_prev)
        + viscosity * (derived_x[1] + derived_y[1] + second_z)
    )
    beta = 4.0 * rows_y * rows_y
    tables_wall = system_tables(
        ((-beta, 1.0 + 2.0 * beta),), rows_y * count_y, place_y * rows_y, rows_y
    )
    solved_wall = solve_reduced(
        explicit[None], tables_wall, "sik,scxkz->scxiz", 3, place_y, count_y, wall_collect
    )
    return (convection, solved_wall[0])


def solution(mesh):
    in_specs = (P(None, "gx", "gy", "gz"), P(None, "gx", "gy", "gz"))
    out_specs = (P(None, "gx", "gy", "gz"), P(None, "gx", "gy", "gz"))
    return jax.shard_map(body, mesh=mesh, in_specs=in_specs, out_specs=out_specs, check_vma=False)
```

profile of v0, /device:TPU:0, one launch (start us, length us, event | category | flops | bytes accessed | tf_op | source)
XLA Modules:
  0.0 699.3 jit_solution(2072480974330309792)
XLA Ops:
  2.4 6.0 collective-permute-start.1
  10.9 82.1 %while.243 = (s32[]{:T(128)}, f32[32]{0:T(128)S(1)}, f32[32,32]{1,0:T(8,128)S(1)}, f32[32,32]{1,0:T(8,128)S(1)}, f32[32]{0:T(128)S(1)}, /*index=5*/f32[32]{0:T(128)S(1)}, s32[]{:T(128)}, s32[]{:T(128)}) while((s32[]{:T(128)}, f32[32]{0:T(128)S(1)}, f32[32,32]{1,0:T(8,128)S(1)}, f32[32,32]{1,0:T(8,128)S(1)}, f32[32]{0:T(128)S(1)}, ...), condition=%wide.region_19.20_spmd.clone, body=%wide.region_18.19_spmd.clone.sunk | while | flops 131 | bytes 783 | solution.py:68
  93.2 79.1 %while.242 = (s32[]{:T(128)}, f32[32]{0:T(128)S(1)}, f32[32,32]{1,0:T(8,128)S(1)}, f32[32,32]{1,0:T(8,128)S(1)}, f32[32]{0:T(128)S(1)}, /*index=5*/f32[32]{0:T(128)S(1)}, s32[]{:T(128)}, s32[]{:T(128)}) while((s32[]{:T(128)}, f32[32]{0:T(128)S(1)}, f32[32,32]{1,0:T(8,128)S(1)}, f32[32,32]{1,0:T(8,128)S(1)}, f32[32]{0:T(128)S(1)}, ...), condition=%wide.region_17.18_spmd.clone, body=%wide.region_16.17_spmd.clone.sunk | while | flops 131 | bytes 783 | solution.py:68
  172.6 41.4 %while.245 = (s32[]{:T(128)}, f32[32]{0:T(128)S(1)}, f32[32,32]{1,0:T(8,128)S(1)}, f32[32,32]{1,0:T(8,128)S(1)}, f32[32]{0:T(128)S(1)}, /*index=5*/s32[]{:T(128)}, s32[]{:T(128)}, s32[]{:T(128)}) while((s32[]{:T(128)}, f32[32]{0:T(128)S(1)}, f32[32,32]{1,0:T(8,128)S(1)}, f32[32,32]{1,0:T(8,128)S(1)}, f32[32]{0:T(128)S(1)}, ...), condition=%wide.region_23.24_spmd.clone, body=%wide.region_22.23_spmd.clone.sunk | while | flops 100 | bytes 779 | solution.py:77
  214.0 42.2 %while.244 = (s32[]{:T(128)}, f32[32]{0:T(128)S(1)}, f32[32,32]{1,0:T(8,128)S(1)}, f32[32,32]{1,0:T(8,128)S(1)}, f32[32]{0:T(128)S(1)}, /*index=5*/s32[]{:T(128)}, s32[]{:T(128)}, s32[]{:T(128)}) while((s32[]{:T(128)}, f32[32]{0:T(128)S(1)}, f32[32,32]{1,0:T(8,128)S(1)}, f32[32,32]{1,0:T(8,128)S(1)}, f32[32]{0:T(128)S(1)}, ...), condition=%wide.region_21.22_spmd.clone, body=%wide.region_20.21_spmd.clone.sunk | while | flops 100 | bytes 779 | solution.py:77
  257.6 41.5 %while.239 = (s32[]{:T(128)}, f32[16]{0:T(128)S(1)}, f32[16,16]{1,0:T(8,128)S(1)}, f32[16,16]{1,0:T(8,128)S(1)}, f32[16]{0:T(128)S(1)}, /*index=5*/f32[16]{0:T(128)S(1)}, s32[]{:T(128)}, s32[]{:T(128)}) while((s32[]{:T(128)}, f32[16]{0:T(128)S(1)}, f32[16,16]{1,0:T(8,128)S(1)}, f32[16,16]{1,0:T(8,128)S(1)}, f32[16]{0:T(128)S(1)}, ...), condition=%wide.region_3.4_spmd.clone, body=%wide.region_2.3_spmd.clone.sunk | while | flops 67 | bytes 463 | solution.py:68
  299.3 41.7 %while.238 = (s32[]{:T(128)}, f32[16]{0:T(128)S(1)}, f32[16,16]{1,0:T(8,128)S(1)}, f32[16,16]{1,0:T(8,128)S(1)}, f32[16]{0:T(128)S(1)}, /*index=5*/f32[16]{0:T(128)S(1)}, s32[]{:T(128)}, s32[]{:T(128)}) while((s32[]{:T(128)}, f32[16]{0:T(128)S(1)}, f32[16,16]{1,0:T(8,128)S(1)}, f32[16,16]{1,0:T(8,128)S(1)}, f32[16]{0:T(128)S(1)}, ...), condition=%wide.region_1.2_spmd.clone, body=%wide.region_0.1_spmd.clone.sunk | while | flops 67 | bytes 463 | solution.py:68
  342.3 21.6 %while.241 = (s32[]{:T(128)}, f32[16]{0:T(128)S(1)}, f32[16,16]{1,0:T(8,128)S(1)}, f32[16,16]{1,0:T(8,128)S(1)}, f32[16]{0:T(128)S(1)}, /*index=5*/s32[]{:T(128)}, s32[]{:T(128)}, s32[]{:T(128)}) while((s32[]{:T(128)}, f32[16]{0:T(128)S(1)}, f32[16,16]{1,0:T(8,128)S(1)}, f32[16,16]{1,0:T(8,128)S(1)}, f32[16]{0:T(128)S(1)}, ...), condition=%wide.region_11.12_spmd.clone, body=%wide.region_10.11_spmd.clone.sunk | while | flops 52 | bytes 459 | solution.py:77
  364.0 19.3 %while.240 = (s32[]{:T(128)}, f32[16]{0:T(128)S(1)}, f32[16,16]{1,0:T(8,128)S(1)}, f32[16,16]{1,0:T(8,128)S(1)}, f32[16]{0:T(128)S(1)}, /*index=5*/s32[]{:T(128)}, s32[]{:T(128)}, s32[]{:T(128)}) while((s32[]{:T(128)}, f32[16]{0:T(128)S(1)}, f32[16,16]{1,0:T(8,128)S(1)}, f32[16,16]{1,0:T(8,128)S(1)}, f32[16]{0:T(128)S(1)}, ...), condition=%wide.region_9.10_spmd.clone, body=%wide.region_8.9_spmd.clone.sunk | while | flops 52 | bytes 459 | solution.py:77
  383.6 79.6 %while.246 = (s32[]{:T(128)}, f32[32]{0:T(128)S(1)}, f32[32,32]{1,0:T(8,128)S(1)}, f32[32,32]{1,0:T(8,128)S(1)}, f32[32]{0:T(128)S(1)}, /*index=5*/f32[32]{0:T(128)S(1)}, s32[]{:T(128)}, s32[]{:T(128)}) while((s32[]{:T(128)}, f32[32]{0:T(128)S(1)}, f32[32,32]{1,0:T(8,128)S(1)}, f32[32,32]{1,0:T(8,128)S(1)}, f32[32]{0:T(128)S(1)}, ...), condition=%wide.region_35.36_spmd.clone, body=%wide.region_34.35_spmd.clone.sunk | while | flops 131 | bytes 783 | solution.py:68
  463.2 42.8 %while.247 = (s32[]{:T(128)}, f32[32]{0:T(128)S(1)}, f32[32,32]{1,0:T(8,128)S(1)}, f32[32,32]{1,0:T(8,128)S(1)}, f32[32]{0:T(128)S(1)}, /*index=5*/s32[]{:T(128)}, s32[]{:T(128)}, s32[]{:T(128)}) while((s32[]{:T(128)}, f32[32]{0:T(128)S(1)}, f32[32,32]{1,0:T(8,128)S(1)}, f32[32,32]{1,0:T(8,128)S(1)}, f32[32]{0:T(128)S(1)}, ...), condition=%wide.region_37.38_spmd.clone, body=%wide.region_36.37_spmd.clone.sunk | while | flops 100 | bytes 779 | solution.py:77
  509.8 2.8 while.237
  521.4 3.2 collective-permute-done.3
  530.1 21.7 %all-reduce.4 = (f32[16]{0:T(128)S(1)}, f32[16]{0:T(128)S(1)}) all-reduce(f32[16]{0:T(128)S(1)} %dynamic-update-slice, f32[16]{0:T(128)S(1)} %dynamic-update-slice.1), channel_id=2, replica_groups=mesh['gx'=8,'gy'=2,'gz'=2] {'gx'}, use_global_device_ids=true, to_apply=%add.2 | all-reduce | flops 32 | bytes 256
  560.4 4.8 maximum_select_fusion
  570.9 5.2 all-gather.4
  577.0 5.1 all-gather.5
  582.7 2.6 fusion.41
  586.5 34.4 %all-gather.1 = f32[16,3,1,32,128]{4,3,2,1,0:T(8,128)} all-gather(f32[2,3,1,32,128]{4,3,2,1,0:T(8,128)S(1)} %bitcast.376), channel_id=3, replica_groups=mesh['gx'=8,'gy'=2,'gz'=2] {'gx'}, dimensions={0}, use_global_device_ids=true | all-gather | bytes 884736 | tf_op jit(solution)/shard_map/all_gather | solution.py:17
  621.0 4.2 fusion.35
  626.4 41.5 %all-gather.3 = f32[16,3,1,32,128]{4,3,2,1,0:T(8,128)} all-gather(f32[2,3,1,32,128]{4,3,2,1,0:T(8,128)S(1)} %bitcast.377), channel_id=5, replica_groups=mesh['gx'=8,'gy'=2,'gz'=2] {'gx'}, dimensions={0}, use_global_device_ids=true | all-gather | bytes 884736 | tf_op jit(solution)/shard_map/all_gather | solution.py:17
  667.9 11.5 %while.233 = (s32[]{:T(128)}, f32[2,3,32,128]{3,2,1,0:T(8,128)S(1)}, s32[]{:T(128)}, f32[8,2,1,1,1]{1,4,3,2,0:T(1,128)}, f32[8,2,3,32,128]{4,3,2,1,0:T(8,128)}, ...) while((s32[]{:T(128)}, f32[2,3,32,128]{3,2,1,0:T(8,128)S(1)}, s32[]{:T(128)}, ...), condition=%wide.region_15.16_spmd, body=%wide.region_14.15_spmd.sunk | while | flops 49158 | bytes 295091 | solution.py:26
  688.4 4.5 all-gather.7
  692.9 4.5 all-gather.6
  (1180 shorter events, 557.0 us)
Async XLA Ops:
  2.3 523.5 %copy-start = (f32[3,16,32,128]{3,1,2,0:T(8,128)}, f32[3,16,32,128]{3,1,2,0:T(8,128)S(1)}, u32[]{:S(2)}) copy-start(f32[3,16,32,128]{3,1,2,0:T(8,128)S(1)} %copy.93) | copy-start | bytes 2359300
  2.4 516.3 %collective-permute-start.1 = (f32[3,3,32,128]{3,1,2,0:T(4,128)S(1)}, f32[3,3,32,128]{3,1,2,0:T(4,128)S(1)}, u32[]{:S(2)}, u32[]{:S(2)}) collective-permute-start(f32[3,3,32,128]{3,1,2,0:T(4,128)S(1)} %get-tuple-element.1564), channel_id=1, source_target_pairs={{4,0},{8,4},{12,8},{16,12},{20,16},{24,20},{28,24},{0,28},{5,1},{9... | collective-permute-start | bytes 442376 | tf_op jit(solution)/shard_map/ppermute | solution.py:38
  8.4 510.3 %collective-permute-start = (f32[3,3,32,128]{3,1,2,0:T(4,128)S(1)}, f32[3,3,32,128]{3,1,2,0:T(4,128)S(1)}, u32[]{:S(2)}, u32[]{:S(2)}) collective-permute-start(f32[3,3,32,128]{3,1,2,0:T(4,128)S(1)} %get-tuple-element.1563), channel_id=1, source_target_pairs={{0,4},{4,8},{8,12},{12,16},{16,20},{20,24},{24,28},{28,0},{1,5},{5... | collective-permute-start | bytes 442376 | tf_op jit(solution)/shard_map/ppermute | solution.py:35
  172.3 343.9 %copy-start.39 = (u32[32]{0:T(128)S(1)}, u32[32]{0:T(128)}, u32[]{:S(2)}) copy-start(u32[32]{0:T(128)} %constant.493) | copy-start | bytes 388
  172.6 84.9 %copy-start.21 = (f32[2,2,2]{2,1,0:T(2,128)}, f32[2,2,2]{2,1,0:T(2,128)S(1)}, u32[]{:S(2)}) copy-start(f32[2,2,2]{2,1,0:T(2,128)S(1)} %get-tuple-element.1075) | copy-start | bytes 100
  299.1 216.1 %copy-start.13 = (f32[16,16]{1,0:T(8,128)}, f32[16,16]{1,0:T(8,128)S(1)}, u32[]{:S(2)}) copy-start(f32[16,16]{1,0:T(8,128)S(1)} %get-tuple-element.1066) | copy-start | bytes 3076
  341.1 42.5 %copy-start.15 = (f32[16,16]{1,0:T(8,128)}, f32[16,16]{1,0:T(8,128)S(1)}, u32[]{:S(2)}) copy-start(f32[16,16]{1,0:T(8,128)S(1)} %get-tuple-element.1065) | copy-start | bytes 3076
  341.5 173.8 %copy-start.24 = (f32[2,16]{1,0:T(2,128)}, f32[2,16]{1,0:T(2,128)S(1)}, u32[]{:S(2)}) copy-start(f32[2,16]{1,0:T(2,128)S(1)} %pad_maximum_fusion.8) | copy-start | bytes 388
  364.0 154.7 %copy-start.17 = (f32[16,16]{1,0:T(8,128)}, f32[16,16]{1,0:T(8,128)S(1)}, u32[]{:S(2)}) copy-start(f32[16,16]{1,0:T(8,128)S(1)} %get-tuple-element.1069) | copy-start | bytes 3076
  383.3 135.4 %copy-start.19 = (f32[16,16]{1,0:T(8,128)}, f32[16,16]{1,0:T(8,128)S(1)}, u32[]{:S(2)}) copy-start(f32[16,16]{1,0:T(8,128)S(1)} %get-tuple-element.1068) | copy-start | bytes 3076
  518.8 5.8 collective-permute-start.3
  520.4 5.4 collective-permute-start.2
  528.4 26.0 %copy-start.8 = (f32[16,32,128]{2,1,0:T(8,128)S(1)}, f32[16,32,128]{2,1,0:T(8,128)}, u32[]{:S(2)}) copy-start(f32[16,32,128]{2,1,0:T(8,128)} %get-tuple-element.1561) | copy-start | bytes 786436
  528.4 26.8 %copy-start.7 = (f32[16,32,128]{2,1,0:T(8,128)S(1)}, f32[16,32,128]{2,1,0:T(8,128)}, u32[]{:S(2)}) copy-start(f32[16,32,128]{2,1,0:T(8,128)} %get-tuple-element.1560) | copy-start | bytes 786436
  528.4 27.7 %copy-start.34 = (f32[32,1]{0,1:T(1,128)S(1)}, f32[32,1]{0,1:T(1,128)}, u32[]{:S(2)}) copy-start(f32[32,1]{0,1:T(1,128)} %negate_bitcast_fusion) | copy-start | bytes 388
  528.4 28.6 %collective-permute-start.5 = (f32[3,22,38,3]{2,1,3,0:T(8,128)}, f32[3,22,38,3]{2,1,3,0:T(8,128)S(1)}, u32[]{:S(2)}, u32[]{:S(2)}) collective-permute-start(f32[3,22,38,3]{2,1,3,0:T(8,128)} %copy.97), channel_id=1, source_target_pairs={{1,0},{0,1},{3,2},{2,3},{5,4},{4,5},{7,6},{6,7},{9,8},{8,9},{11,10... | collective-permute-start | bytes 90296 | tf_op jit(solution)/shard_map/ppermute | solution.py:38
  529.0 29.7 %collective-permute-start.4 = (f32[3,22,38,3]{2,1,3,0:T(8,128)S(1)}, f32[3,22,38,3]{2,1,3,0:T(8,128)S(1)}, u32[]{:S(2)}, u32[]{:S(2)}) collective-permute-start(f32[3,22,38,3]{2,1,3,0:T(8,128)S(1)} %copy.96), channel_id=1, source_target_pairs={{0,1},{1,0},{2,3},{3,2},{4,5},{5,4},{6,7},{7,6},{8,9},{9,8},{10,11... | collective-permute-start | bytes 90296 | tf_op jit(solution)/shard_map/ppermute | solution.py:35
  585.3 35.7 %copy-start.18 = (f32[16,16]{1,0:T(8,128)S(1)}, f32[16,16]{1,0:T(8,128)}, u32[]{:S(2)}) copy-start(f32[16,16]{1,0:T(8,128)} %copy-done.17) | copy-start | bytes 3076
  585.3 35.7 %copy-start.20 = (f32[16,16]{1,0:T(8,128)S(1)}, f32[16,16]{1,0:T(8,128)}, u32[]{:S(2)}) copy-start(f32[16,16]{1,0:T(8,128)} %copy-done.19) | copy-start | bytes 3076
  585.3 35.7 %copy-start.25 = (f32[2,16]{1,0:T(2,128)S(1)}, f32[2,16]{1,0:T(2,128)}, u32[]{:S(2)}) copy-start(f32[2,16]{1,0:T(2,128)} %copy-done.24) | copy-start | bytes 388
  625.2 54.2 %copy-start.27 = (f32[2,16]{1,0:T(2,128)S(1)}, f32[2,16]{1,0:T(2,128)}, u32[]{:S(2)}) copy-start(f32[2,16]{1,0:T(2,128)} %copy-done.26) | copy-start | bytes 388
  686.5 11.3 %copy-start.38 = (f32[2,1,2]{2,1,0:T(1,128)S(1)}, f32[2,1,2]{2,1,0:T(1,128)}, u32[]{:S(2)}) copy-start(f32[2,1,2]{2,1,0:T(1,128)} %copy-done.37) | copy-start | bytes 52
  686.5 11.7 %copy-start.29 = (f32[32]{0:T(128)S(1)}, f32[32]{0:T(128)}, u32[]{:S(2)}) copy-start(f32[32]{0:T(128)} %convolution_bitcast_fusion.1) | copy-start | bytes 388
  686.5 11.7 %copy-start.32 = (f32[32]{0:T(128)S(1)}, f32[32]{0:T(128)}, u32[]{:S(2)}) copy-start(f32[32]{0:T(128)} %rev.39) | copy-start | bytes 388
  (22 other events, 89.7 us)
where the time goes:
time: 703 us; the launch traced here: 699 us
  local copies, waits for them, and re-layouts  278 us (40%)
  other arithmetic  269 us (38%)
  blocking collectives  117 us (17%)
  matrix products  15.2 us (2%)
  starting transfers between devices  8.68 us (1%)
    dynamic_slice x384, local copies, waits for them, and re-layouts, block_tables(): lax.scan(forward_row, jnp.zeros((length,), jnp.float32), (ratio, pivot, u...  238 us
    sub x128, other arithmetic, forward_row(): fresh = unit_row / pivot_now - ratio_now * carry  158 us
    sub x128, other arithmetic, backward_row(): fresh = unit_row - ratio_now * carry  80.9 us
    all_gather x2, blocking collectives, entering(): gathered = jax.tree.map(lambda a: lax.all_gather(a, axis), part)  75.9 us
    unnamed x1, blocking collectives  21.7 us
  transfers between devices with their start and end apart: 6, of which 2 were waited for; matrix products, arithmetic and copies ran while one was open for 73% of the time, Pallas kernels for 0%

commit v1 on v0

v1 whole, which is shorter than its diff:
```python
import collections
import functools

import jax
import jax.numpy as jnp
import numpy as np
from jax import lax
from jax.experimental import pallas as pl
from jax.experimental.pallas import tpu as pltpu
from jax.sharding import PartitionSpec as P

MESH = pl.DeviceIdType.MESH
time_step = 1.0
gamma_now = 5.0 / 12.0
zeta_old = -17.0 / 60.0
viscosity = 0.1

FIRST = {1: 7.0 / 9.0, -1: -7.0 / 9.0, 2: 1.0 / 36.0, -2: -1.0 / 36.0}
SECOND = {1: 12.0 / 11.0, -1: 12.0 / 11.0, 2: 3.0 / 44.0, -2: 3.0 / 44.0, 0: -24.0 / 11.0 - 6.0 / 44.0}
COMPACT = ((1.0 / 3.0, 1.0, FIRST), (2.0 / 11.0, 1.0, SECOND))


class System:
    def __init__(self, off, mid, stencil, count, m):
        n = count * m
        rho = np.zeros(n + 2)
        last = 0.0
        for j in range(n + 2):
            last = -off / (mid + off * last)
            rho[j] = last

        def u(j, ref):
            if j < 0:
                return 0.0
            if j <= ref:
                return float(np.prod(rho[j:ref]))
            return 1.0 / float(np.prod(rho[ref:j]))

        def v(j, ref):
            return u(n - 1 - j, n - 1 - ref)

        def inv(i, j):
            low = rho[i - 1] if i > 0 else 0.0
            high = rho[n - 2 - i] if i < n - 1 else 0.0
            diag = 1.0 / (mid + off * low + off * high)
            return diag * (u(j, i) if j <= i else v(j, i))

        def b(j, col):
            return stencil.get(col - j, 0.0)

        self.off, self.m, self.count = off, m, count
        self.right, self.left = np.zeros((count, m)), np.zeros((count, m))
        self.fix_low, self.fix_high = np.zeros((count, 3)), np.zeros((count, 3))
        self.d = np.zeros((count, 4))
        self.t = np.zeros((count, 2))
        self.weights = np.zeros((2, count, 2, count))
        for p in range(count):
            start, end = p * m, p * m + m - 1
            for k in range(m):
                col = start + k
                rows = [j for j in range(col - 2, col + 3) if 0 <= j < n]
                self.right[p, k] = sum(u(j, end) * b(j, col) for j in rows)
                self.left[p, k] = sum(v(j, start) * b(j, col) for j in rows)
            if p > 0:
                e = start - 1
                self.fix_low[p] = (
                    sum((inv(e, j) - inv(e, e) * u(j, e)) * b(j, e) for j in (e + 1, e + 2)),
                    (inv(e, e + 1) - inv(e, e) * u(e + 1, e)) * b(e + 1, e - 1),
                    (inv(e, e - 1) - inv(e, e + 1) * v(e - 1, e + 1)) * b(e - 1, e + 1),
                )
                self.d[p, 0], self.d[p, 1] = inv(e, e), inv(e, e + 1)
                self.t[p, 0] = u(e, end)
                for q in range(count):
                    if q < p:
                        self.weights[0, q, 0, p] = inv(e, q * m + m - 1)
                    else:
                        self.weights[0, q, 1, p] = inv(e, q * m)
            if p < count - 1:
                f = end + 1
                self.fix_high[p] = (
                    sum((inv(f, j) - inv(f, f) * v(j, f)) * b(j, f) for j in (f - 1, f - 2)),
                    (inv(f, f - 1) - inv(f, f) * v(f - 1, f)) * b(f - 1, f + 1),
                    (inv(f, f + 1) - inv(f, f - 1) * u(f + 1, f - 1)) * b(f + 1, f - 1),
                )
                self.d[p, 2], self.d[p, 3] = inv(f, f - 1), inv(f, f)
                self.t[p, 1] = v(f, start)
                for q in range(count):
                    if q > p:
                        self.weights[1, q, 1, p] = inv(f, q * m)
                    else:
                        self.weights[1, q, 0, p] = inv(f, q * m + m - 1)
        pivots, ratios, last = [], [], 0.0
        for _ in range(m):
            pivot = mid - off * last
            last = off / pivot
            pivots.append(pivot)
            ratios.append(last)
        self.scale = [float(1.0 / pivot) for pivot in pivots]
        self.ratio = [float(ratio) for ratio in ratios]
        unit = np.zeros(m)
        unit[0] = 1.0
        self.low = [-off * value for value in self.solve(list(unit))]
        self.high = self.low[::-1]

    def solve(self, rows):
        done, carry = [], None
        for i, row in enumerate(rows):
            fresh = row * self.scale[i]
            carry = fresh if carry is None else fresh - self.ratio[i] * carry
            done.append(carry)
        for i in range(self.m - 2, -1, -1):
            done[i] = done[i] - self.ratio[i] * done[i + 1]
        return done


def pick(place, values):
    values = [float(np.float32(value)) for value in values]
    common = collections.Counter(values).most_common(1)[0][0]
    result = jnp.float32(common)
    for index, value in enumerate(values):
        if value != common:
            result = jnp.where(place == index, jnp.float32(value), result)
    return result


def sides(at):
    odd_1, even_1 = at(1) - at(-1), at(1) + at(-1)
    odd_2, even_2 = at(2) - at(-2), at(2) + at(-2)
    first = FIRST[1] * odd_1 + FIRST[2] * odd_2
    second = SECOND[1] * even_1 + (SECOND[2] * even_2 + SECOND[0] * at(0))
    return first, second


def total(terms):
    return functools.reduce(lambda a, b: a + b, terms)


def kernel(
    cfg, v, cp, conv, upd,
    zo, xlo, xhi, ypack, ylo, yhi, gx, gr, to, ti, gy, gyr, gw, gwr,
    fx, sx, fy, sy, expl,
    t1s, t1r, t2s, t2r, xs, xr, ys, yr, gys, gyrs, ws, wr, zs, zr,
):
    nc, mx, my, nz, px, py, units = cfg
    real = len(COMPACT) * nc * (my // 8)
    me = lax.axis_index("gx")
    wall = lax.axis_index("gy")
    core = lax.axis_index("gz")
    sys_x = [System(*pair, px, mx) for pair in COMPACT]
    sys_y = [System(*pair, py, my) for pair in COMPACT]
    beta = 4.0 * my * my
    sys_w = System(-beta, 1.0 + 2.0 * beta, {0: 1.0}, py, my)

    def gx_peer(d):
        return lax.rem(me + d, px)

    def gy_peer(d):
        return lax.rem(wall + d, py)

    barrier = pltpu.get_barrier_semaphore()
    for d in range(1, px):
        pl.semaphore_signal(barrier, inc=1, device_id={"gx": gx_peer(d)}, device_id_type=MESH)
    for d in range(1, py):
        pl.semaphore_signal(barrier, inc=1, device_id={"gy": gy_peer(d)}, device_id_type=MESH)
    pl.semaphore_signal(barrier, inc=1, device_id={"gz": 1 - core}, device_id_type=MESH)

    def remote(src, dst, send, recv, **target):
        return pltpu.make_async_remote_copy(
            src_ref=src, dst_ref=dst, send_sem=send, recv_sem=recv,
            device_id=target, device_id_type=MESH,
        )

    per = nc * (my // 8)
    for s in range(2):
        right = [pick(me, sys_x[s].right[:, i]) for i in range(mx)]
        left = [pick(me, sys_x[s].left[:, i]) for i in range(mx)]

        def sums_x(c, _, s=s, right=right, left=left):
            rows = [v[c, pl.ds(i * my, my), :] for i in range(mx)]
            for way, table in ((0, right), (1, left)):
                value = total([table[i] * rows[i] for i in range(mx)])
                gx[way, pl.ds(s * per + c * (my // 8), my // 8)] = value.reshape(my // 8, 8, nz)
            return 0

        lax.fori_loop(0, nc, sums_x, 0)
    if px * units > real:
        gx[:, pl.ds(real, px * units - real)] = jnp.zeros((2, px * units - real, 8, nz), jnp.float32)

    pl.semaphore_wait(barrier, px - 1 + py - 1 + 1)

    first_round = []
    for d in range(1, px):
        t = gx_peer(d)
        source = gx_peer(px - d)
        copy = remote(
            gx.at[:, pl.ds(t * units, units)], gr.at[me], t1s.at[d], t1r.at[d], gx=t
        )
        copy.start()
        first_round.append((copy, source))
    gr[me] = gx[:, pl.ds(me * units, units)]

    up = remote(v.at[:, pl.ds((mx - 2) * my, 2 * my)], xlo, xs.at[0], xr.at[0], gx=gx_peer(1))
    down = remote(v.at[:, pl.ds(0, 2 * my)], xhi, xs.at[1], xr.at[1], gx=gx_peer(px - 1))

    @pl.when(me < px - 1)
    def _():
        up.start()

    @pl.when(me > 0)
    def _():
        down.start()

    z_copies = []
    for c in range(nc):
        copy = remote(v.at[c], zo.at[c], zs.at[c], zr.at[c], gz=1 - core)
        copy.start()
        z_copies.append(copy)

    def yrow(ref, c, y):
        return ref[c, pl.ds(y, mx, stride=my), :]

    for c in range(nc):
        for side, first in ((0, my - 2), (1, 0)):
            for k in range(2):
                ypack[side, k, c] = yrow(v, c, first + k)
    y_up = remote(ypack.at[0], ylo, ys.at[0], yr.at[0], gy=gy_peer(1))
    y_down = remote(ypack.at[1], yhi, ys.at[1], yr.at[1], gy=gy_peer(py - 1))

    @pl.when(wall < py - 1)
    def _():
        y_up.start()

    @pl.when(wall > 0)
    def _():
        y_down.start()

    for s in range(2):
        right = [pick(wall, sys_y[s].right[:, i]) for i in range(my)]
        left = [pick(wall, sys_y[s].left[:, i]) for i in range(my)]

        def sums_y(c, _, s=s, right=right, left=left):
            low = high = None
            for i in range(my):
                row = yrow(v, c, i)
                low = right[i] * row if low is None else low + right[i] * row
                high = left[i] * row if high is None else high + left[i] * row
            gy[0, s, c] = low
            gy[1, s, c] = high
            return 0

        lax.fori_loop(0, nc, sums_y, 0)
    gy_copies = []
    for d in range(1, py):
        copy = remote(gy, gyr.at[wall], gys.at[d], gyrs.at[d], gy=gy_peer(d))
        copy.start()
        gy_copies.append(copy)
    gyr[wall] = gy[...]

    @pl.when(me > 0)
    def _():
        up.wait_recv()

    @pl.when(me == 0)
    def _():
        xlo[...] = jnp.zeros_like(xlo)

    @pl.when(me < px - 1)
    def _():
        down.wait_recv()

    @pl.when(me == px - 1)
    def _():
        xhi[...] = jnp.zeros_like(xhi)

    low_x = [[pick(me, -s.off * s.fix_low[:, k]) for k in range(3)] for s in sys_x]
    high_x = [[pick(me, -s.off * s.fix_high[:, k]) for k in range(3)] for s in sys_x]
    tile = 16 if my % 16 == 0 else 8

    def solve_x(index, _):
        c = index // (my // tile)
        base = lax.rem(index, my // tile) * tile
        rows = [xlo[c, pl.ds(k * my + base, tile), :] for k in range(2)]
        rows += [v[c, pl.ds(i * my + base, tile), :] for i in range(mx)]
        rows += [xhi[c, pl.ds(k * my + base, tile), :] for k in range(2)]
        pairs = [sides(lambda k, i=i: rows[i + 2 + k]) for i in range(mx)]
        for s, out in ((0, fx), (1, sx)):
            rhs = [pair[s] for pair in pairs]
            rhs[0] = rhs[0] + (
                low_x[s][0] * rows[1] + low_x[s][1] * rows[0] + low_x[s][2] * rows[2]
            )
            rhs[mx - 1] = rhs[mx - 1] + (
                high_x[s][0] * rows[mx + 2] + high_x[s][1] * rows[mx + 3] + high_x[s][2] * rows[mx + 1]
            )
            for i, value in enumerate(sys_x[s].solve(rhs)):
                out[c, pl.ds(i * my + base, tile), :] = value
        return 0

    lax.fori_loop(0, nc * (my // tile), solve_x, 0)

    for copy, _ in first_round:
        copy.wait_recv()
    share = jnp.minimum(me * units // per, 1)

    def both(field):
        return [pick(share, [field(sys_x[0], p), field(sys_x[1], p)]) for p in range(px)]

    t0, t1 = (both(lambda s, p, k=k: s.t[p, k]) for k in range(2))
    d0, d1, d2, d3 = (both(lambda s, p, k=k: s.d[p, k]) for k in range(4))
    below, above = [None] * px, [None] * px
    for p in range(px):
        here = gr[p, 0]
        below[p] = here if p == 0 else here + t0[p] * below[p - 1]
    for p in reversed(range(px)):
        here = gr[p, 1]
        above[p] = here if p == px - 1 else here + t1[p] * above[p + 1]
    for p in range(px):
        zero = jnp.zeros((units, 8, nz), jnp.float32)
        to[p, 0] = zero if p == 0 else d0[p] * below[p - 1] + d1[p] * above[p]
        to[p, 1] = zero if p == px - 1 else d2[p] * below[p] + d3[p] * above[p + 1]
    second_round = []
    for d in range(1, px):
        t = gx_peer(d)
        copy = remote(to.at[t], ti.at[:, pl.ds(me * units, units)], t2s.at[d], t2r.at[d], gx=t)
        copy.start()
        second_round.append(copy)
    ti[:, pl.ds(me * units, units)] = to[me]

    @pl.when(wall > 0)
    def _():
        y_up.wait_recv()

    @pl.when(wall == 0)
    def _():
        ylo[...] = jnp.zeros_like(ylo)

    @pl.when(wall < py - 1)
    def _():
        y_down.wait_recv()

    @pl.when(wall == py - 1)
    def _():
        yhi[...] = jnp.zeros_like(yhi)

    for copy in gy_copies:
        copy.wait_recv()

    def gathered(system, side):
        return [[pick(wall, system.weights[side, q, way]) for way in range(2)] for q in range(py)]

    low_y = [[pick(wall, -s.off * s.fix_low[:, k]) for k in range(3)] for s in sys_y]
    high_y = [[pick(wall, -s.off * s.fix_high[:, k]) for k in range(3)] for s in sys_y]
    outer_y = [[gathered(s, side) for side in range(2)] for s in sys_y]

    def solve_y(index, _):
        c = index // (mx // 8)
        base = lax.rem(index, mx // 8) * 8
        part = pl.ds(base, 8)
        rows = [ylo[k, c, part, :] for k in range(2)]
        rows += [v[c, pl.ds(base * my + y, 8, stride=my), :] for y in range(my)]
        rows += [yhi[k, c, part, :] for k in range(2)]
        pairs = [sides(lambda k, i=i: rows[i + 2 + k]) for i in range(my)]
        for s, out in ((0, fy), (1, sy)):
            rhs = [pair[s] for pair in pairs]
            ends = [
                total([
                    outer_y[s][side][q][way] * gyr[q, way, s, c, part, :]
                    for q in range(py) for way in range(2)
                ])
                for side in range(2)
            ]
            rhs[0] = rhs[0] + (
                low_y[s][0] * rows[1] + low_y[s][1] * rows[0] + low_y[s][2] * rows[2]
                - sys_y[s].off * ends[0]
            )
            rhs[my - 1] = rhs[my - 1] + (
                high_y[s][0] * rows[my + 2] + high_y[s][1] * rows[my + 3] + high_y[s][2] * rows[my + 1]
                - sys_y[s].off * ends[1]
            )
            for i, value in enumerate(sys_y[s].solve(rhs)):
                out[c, pl.ds(base * my + i, 8, stride=my), :] = value
        return 0

    lax.fori_loop(0, nc * (mx // 8), solve_y, 0)

    for copy in z_copies:
        copy.wait_recv()

    def solve_z(index, _):
        c = index // mx
        part = pl.ds(lax.rem(index, mx) * my, my)
        own, other = v[c, part, :], zo[c, part, :]
        lane = lax.broadcasted_iota(jnp.int32, own.shape, 1)

        def ahead(k):
            return pltpu.roll(jnp.where(lane < k, other, own), nz - k, 1)

        def back(k):
            return pltpu.roll(jnp.where(lane >= nz - k, other, own), k, 1)

        p1, m1, p2, m2, p3, m3 = ahead(1), back(1), ahead(2), back(2), ahead(3), back(3)
        first = (45.0 / 60.0) * (p1 - m1) - (9.0 / 60.0) * (p2 - m2) + (1.0 / 60.0) * (p3 - m3)
        second = (
            (2.0 / 180.0) * (p3 + m3) - (27.0 / 180.0) * (p2 + m2)
            + (270.0 / 180.0) * (p1 + m1) - (490.0 / 180.0) * own
        )
        moved = v[0, part, :] * fx[c, part, :] + v[1, part, :] * fy[c, part, :] + v[2, part, :] * first
        conv[c, part, :] = moved
        expl[c, part, :] = (
            own - time_step * (gamma_now * moved + zeta_old * cp[c, part, :])
            + viscosity * (sx[c, part, :] + sy[c, part, :] + second)
        )
        return 0

    lax.fori_loop(0, nc * mx, solve_z, 0)

    for copy in second_round:
        copy.wait_recv()
    for c in range(nc):
        lines = my // 8
        outer = [
            [ti[way, pl.ds(s * per + c * lines, lines)].reshape(my, nz) for way in range(2)]
            for s in range(2)
        ]
        for i in range(mx):
            part = pl.ds(i * my, my)
            more = sys_x[0].low[i] * outer[0][0] + sys_x[0].high[i] * outer[0][1]
            bend = sys_x[1].low[i] * outer[1][0] + sys_x[1].high[i] * outer[1][1]
            moved = v[0, part, :] * more
            conv[c, part, :] = conv[c, part, :] + moved
            expl[c, part, :] = expl[c, part, :] + (viscosity * bend - (time_step * gamma_now) * moved)

    right_w = [pick(wall, sys_w.right[:, i]) for i in range(my)]
    left_w = [pick(wall, sys_w.left[:, i]) for i in range(my)]

    def sums_w(c, _):
        low = high = None
        for i in range(my):
            row = yrow(expl, c, i)
            low = right_w[i] * row if low is None else low + right_w[i] * row
            high = left_w[i] * row if high is None else high + left_w[i] * row
        gw[0, c] = low
        gw[1, c] = high
        return 0

    lax.fori_loop(0, nc, sums_w, 0)
    w_copies = []
    for d in range(1, py):
        copy = remote(gw, gwr.at[wall], ws.at[d], wr.at[d], gy=gy_peer(d))
        copy.start()
        w_copies.append(copy)
    gwr[wall] = gw[...]

    def solve_w(index, _):
        c = index // (mx // 8)
        base = lax.rem(index, mx // 8) * 8
        rows = [expl[c, pl.ds(base * my + y, 8, stride=my), :] for y in range(my)]
        for i, value in enumerate(sys_w.solve(rows)):
            upd[c, pl.ds(base * my + i, 8, stride=my), :] = value
        return 0

    lax.fori_loop(0, nc * (mx // 8), solve_w, 0)
    for copy in w_copies:
        copy.wait_recv()
    outer_w = [gathered(sys_w, side) for side in range(2)]

    def finish(c, _):
        ends = [
            total([
                outer_w[side][q][way] * gwr[q, way, c] for q in range(py) for way in range(2)
            ])
            for side in range(2)
        ]
        for i in range(my):
            at = pl.ds(i, mx, stride=my)
            upd[c, at, :] = upd[c, at, :] + (sys_w.low[i] * ends[0] + sys_w.high[i] * ends[1])
        return 0

    lax.fori_loop(0, nc, finish, 0)

    for copy, _ in first_round:
        copy.wait_send()
    for copy in second_round + z_copies + gy_copies + w_copies:
        copy.wait_send()

    @pl.when(me < px - 1)
    def _():
        up.wait_send()

    @pl.when(me > 0)
    def _():
        down.wait_send()

    @pl.when(wall < py - 1)
    def _():
        y_up.wait_send()

    @pl.when(wall > 0)
    def _():
        y_down.wait_send()


def body(counts, velocity, conv_prev):
    px, py, pz = counts
    nc, mx, my, nz = velocity.shape
    assert pz == 2 and my % 8 == 0 and mx % 8 == 0
    real = 2 * nc * (my // 8)
    units = -(-real // px)
    assert (real // 2) % units == 0
    flat = (nc, mx * my, nz)
    f32 = jnp.float32

    def vmem(*shape):
        return pltpu.VMEM(shape, f32)

    def dma(n):
        return pltpu.SemaphoreType.DMA((n,))

    whole = pl.BlockSpec(memory_space=pltpu.VMEM)
    conv, upd = pl.pallas_call(
        functools.partial(kernel, (nc, mx, my, nz, px, py, units)),
        out_shape=[jax.ShapeDtypeStruct(flat, f32)] * 2,
        in_specs=[whole, whole],
        out_specs=[whole, whole],
        scratch_shapes=[
            vmem(*flat),
            vmem(nc, 2 * my, nz), vmem(nc, 2 * my, nz),
            vmem(2, 2, nc, mx, nz), vmem(2, nc, mx, nz), vmem(2, nc, mx, nz),
            vmem(2, px * units, 8, nz), vmem(px, 2, units, 8, nz),
            vmem(px, 2, units, 8, nz), vmem(2, px * units, 8, nz),
            vmem(2, 2, nc, mx, nz), vmem(py, 2, 2, nc, mx, nz),
            vmem(2, nc, mx, nz), vmem(py, 2, nc, mx, nz),
            vmem(*flat), vmem(*flat), vmem(*flat), vmem(*flat), vmem(*flat),
            dma(px), dma(px), dma(px), dma(px), dma(2), dma(2), dma(2), dma(2),
            dma(py), dma(py), dma(py), dma(py), dma(nc), dma(nc),
        ],
        compiler_params=pltpu.CompilerParams(
            collective_id=0, has_side_effects=True, vmem_limit_bytes=32 * 1024 * 1024
        ),
    )(velocity.reshape(flat), conv_prev.reshape(flat))
    return conv.reshape(velocity.shape), upd.reshape(velocity.shape)


def solution(mesh):
    spec = P(None, "gx", "gy", "gz")
    counts = tuple(mesh.shape[name] for name in ("gx", "gy", "gz"))
    return jax.shard_map(
        functools.partial(body, counts), mesh=mesh, in_specs=(spec, spec),
        out_specs=(spec, spec), check_vma=False,
    )
```

time: 703 us -> 30.7 us (0.04)
  the two profiles are of different devices: /device:TPU:0 before, /device:TPU:2 now
where the time goes in v1:
time: 30.7 us; the launch traced here: 30.5 us
  Pallas kernels  25.9 us (84%)
  local copies, waits for them, and re-layouts  4.02 us (13%)
  between operations  0.65 us (2%)
    pallas_call x1, Pallas kernels, body(): pl.pallas_call(functools.partial(kernel, (nc, mx, my, nz, px, py, units))...  25.9 us
    unnamed x6, local copies, waits for them, and re-layouts  4.02 us

profile of v1, /device:TPU:2, one launch (start us, length us, event | category | flops | bytes accessed | tf_op | source)
XLA Modules:
  0.0 30.5 jit_solution(7800144304009021215)
XLA Ops:
  0.6 0.0 copy-start
  0.6 1.1 %copy-done = f32[3,16,32,128]{3,2,1,0:T(8,128)S(1)} copy-done((f32[3,16,32,128]{3,2,1,0:T(8,128)S(1)}, f32[3,16,32,128]{3,2,1,0:T(8,128)}, u32[]{:S(2)}) %copy-start) | copy-done | bytes 786456
  1.8 0.0 copy-start.1
  1.8 1.1 %copy-done.1 = f32[3,16,32,128]{3,2,1,0:T(8,128)S(1)} copy-done((f32[3,16,32,128]{3,2,1,0:T(8,128)S(1)}, f32[3,16,32,128]{3,2,1,0:T(8,128)}, u32[]{:S(2)}) %copy-start.1) | copy-done | bytes 786456
  2.9 25.9 %shard_map.41 = (f32[3,512,128]{2,1,0:T(8,128)S(1)}, f32[3,512,128]{2,1,0:T(8,128)S(1)}) custom-call(f32[3,512,128]{2,1,0:T(8,128)S(1)} %bitcast.4, f32[3,512,128]{2,1,0:T(8,128)S(1)} %bitcast.5), custom_call_target="tpu_custom_call" | custom-call | tf_op jit(solution)/shard_map/pallas_call | solution.py:519
  28.8 0.9 %copy.6 = f32[3,16,32,128]{3,2,1,0:T(8,128)} copy(f32[3,16,32,128]{3,2,1,0:T(8,128)S(1)} %bitcast.7) | data formatting | bytes 1572864
  29.7 0.9 %copy.7 = f32[3,16,32,128]{3,2,1,0:T(8,128)} copy(f32[3,16,32,128]{3,2,1,0:T(8,128)S(1)} %bitcast.6) | data formatting | bytes 1572864
Async XLA Ops:
  0.6 1.1 %copy-start = (f32[3,16,32,128]{3,2,1,0:T(8,128)S(1)}, f32[3,16,32,128]{3,2,1,0:T(8,128)}, u32[]{:S(2)}) copy-start(f32[3,16,32,128]{3,2,1,0:T(8,128)} %param.2) | copy-start | bytes 2359300
  1.8 1.1 %copy-start.1 = (f32[3,16,32,128]{3,2,1,0:T(8,128)S(1)}, f32[3,16,32,128]{3,2,1,0:T(8,128)}, u32[]{:S(2)}) copy-start(f32[3,16,32,128]{3,2,1,0:T(8,128)} %param.3) | copy-start | bytes 2359300

commit v2 on v1

--- a/solution.py
+++ b/solution.py
@@ -10,6 +10,7 @@
 from jax.sharding import PartitionSpec as P
 
 MESH = pl.DeviceIdType.MESH
+WIDE = 8
 time_step = 1.0
 gamma_now = 5.0 / 12.0
 zeta_old = -17.0 / 60.0
@@ -136,9 +137,10 @@
 
 
 def kernel(
-    cfg, v, cp, conv, upd,
-    zo, xlo, xhi, ypack, ylo, yhi, gx, gr, to, ti, gy, gyr, gw, gwr,
-    fx, sx, fy, sy, expl,
+    cfg, v_hbm, cp_hbm, conv, upd,
+    v, cp, load,
+    wz, vt, zo, xlo, xhi, ylo, yhi, gx, gr, to, ti, gy, gyr, gw, gwr,
+    fx, sx, fy, sy, expl, et,
     t1s, t1r, t2s, t2r, xs, xr, ys, yr, gys, gyrs, ws, wr, zs, zr,
 ):
     nc, mx, my, nz, px, py, units = cfg
@@ -151,6 +153,11 @@
     beta = 4.0 * my * my
     sys_w = System(-beta, 1.0 + 2.0 * beta, {0: 1.0}, py, my)
 
+    reads = [pltpu.make_async_copy(v_hbm.at[c], v.at[c], load.at[c]) for c in range(nc)]
+    reads_cp = [pltpu.make_async_copy(cp_hbm.at[c], cp.at[c], load.at[nc + c]) for c in range(nc)]
+    for read in reads + reads_cp:
+        read.start()
+
     def gx_peer(d):
         return lax.rem(me + d, px)
 
@@ -170,21 +177,40 @@
             device_id=target, device_id_type=MESH,
         )
 
+    for read in reads:
+        read.wait()
+
     per = nc * (my // 8)
-    for s in range(2):
-        right = [pick(me, sys_x[s].right[:, i]) for i in range(mx)]
-        left = [pick(me, sys_x[s].left[:, i]) for i in range(mx)]
-
-        def sums_x(c, _, s=s, right=right, left=left):
-            rows = [v[c, pl.ds(i * my, my), :] for i in range(mx)]
-            for way, table in ((0, right), (1, left)):
-                value = total([table[i] * rows[i] for i in range(mx)])
+    weigh_x = [
+        [[pick(me, table[:, i]) for i in range(mx)] for table in (s.right, s.left)] for s in sys_x
+    ]
+
+    def sums_x(c, _):
+        rows = [v[c, pl.ds(i * my, my), :] for i in range(mx)]
+        for s in range(2):
+            for way in range(2):
+                value = total([weigh_x[s][way][i] * rows[i] for i in range(mx)])
                 gx[way, pl.ds(s * per + c * (my // 8), my // 8)] = value.reshape(my // 8, 8, nz)
-            return 0
-
-        lax.fori_loop(0, nc, sums_x, 0)
+        return 0
+
+    lax.fori_loop(0, nc, sums_x, 0)
     if px * units > real:
         gx[:, pl.ds(real, px * units - real)] = jnp.zeros((2, px * units - real, 8, nz), jnp.float32)
+
+    size = (2 * nz, 2 * nz)
+    source = lax.broadcasted_iota(jnp.int32, size, 0)
+    target = lax.broadcasted_iota(jnp.int32, size, 1)
+    is_first = target < nz
+    gap = source - jnp.where(is_first, target, target - nz)
+    gap = jnp.where((source >= nz) & (gap > nz), gap - 2 * nz, gap)
+    far = jnp.abs(gap)
+    odd = jnp.where(far == 1, 45.0, jnp.where(far == 2, -9.0, jnp.where(far == 3, 1.0, 0.0)))
+    odd = jnp.where(gap < 0, -odd, odd)
+    even = jnp.where(
+        far == 0, -490.0,
+        jnp.where(far == 1, 270.0, jnp.where(far == 2, -27.0, jnp.where(far == 3, 2.0, 0.0))),
+    )
+    wz[...] = jnp.where(is_first, odd, even).astype(jnp.bfloat16)
 
     pl.semaphore_wait(barrier, px - 1 + py - 1 + 1)
 
@@ -219,12 +245,27 @@
     def yrow(ref, c, y):
         return ref[c, pl.ds(y, mx, stride=my), :]
 
-    for c in range(nc):
-        for side, first in ((0, my - 2), (1, 0)):
-            for k in range(2):
-                ypack[side, k, c] = yrow(v, c, first + k)
-    y_up = remote(ypack.at[0], ylo, ys.at[0], yr.at[0], gy=gy_peer(1))
-    y_down = remote(ypack.at[1], yhi, ys.at[1], yr.at[1], gy=gy_peer(py - 1))
+    weigh_y = [
+        [[pick(wall, table[:, i]) for i in range(my)] for table in (s.right, s.left)] for s in sys_y
+    ]
+
+    def sums_y(c, _):
+        sums = [[None, None], [None, None]]
+        for i in range(my):
+            row = yrow(v, c, i)
+            vt[c, i] = row
+            for s in range(2):
+                for way in range(2):
+                    term = weigh_y[s][way][i] * row
+                    sums[s][way] = term if i == 0 else sums[s][way] + term
+        for s in range(2):
+            for way in range(2):
+                gy[way, s, c] = sums[s][way]
+        return 0
+
+    lax.fori_loop(0, nc, sums_y, 0)
+    y_up = remote(vt.at[:, pl.ds(my - 2, 2)], ylo, ys.at[0], yr.at[0], gy=gy_peer(1))
+    y_down = remote(vt.at[:, pl.ds(0, 2)], yhi, ys.at[1], yr.at[1], gy=gy_peer(py - 1))
 
     @pl.when(wall < py - 1)
     def _():
@@ -234,21 +275,6 @@
     def _():
         y_down.start()
 
-    for s in range(2):
-        right = [pick(wall, sys_y[s].right[:, i]) for i in range(my)]
-        left = [pick(wall, sys_y[s].left[:, i]) for i in range(my)]
-
-        def sums_y(c, _, s=s, right=right, left=left):
-            low = high = None
-            for i in range(my):
-                row = yrow(v, c, i)
-                low = right[i] * row if low is None else low + right[i] * row
-                high = left[i] * row if high is None else high + left[i] * row
-            gy[0, s, c] = low
-            gy[1, s, c] = high
-            return 0
-
-        lax.fori_loop(0, nc, sums_y, 0)
     gy_copies = []
     for d in range(1, py):
         copy = remote(gy, gyr.at[wall], gys.at[d], gyrs.at[d], gy=gy_peer(d))
@@ -256,46 +282,64 @@
         gy_copies.append(copy)
     gyr[wall] = gy[...]
 
-    @pl.when(me > 0)
-    def _():
-        up.wait_recv()
-
-    @pl.when(me == 0)
-    def _():
-        xlo[...] = jnp.zeros_like(xlo)
-
-    @pl.when(me < px - 1)
-    def _():
-        down.wait_recv()
-
-    @pl.when(me == px - 1)
-    def _():
-        xhi[...] = jnp.zeros_like(xhi)
-
-    low_x = [[pick(me, -s.off * s.fix_low[:, k]) for k in range(3)] for s in sys_x]
-    high_x = [[pick(me, -s.off * s.fix_high[:, k]) for k in range(3)] for s in sys_x]
-    tile = 16 if my % 16 == 0 else 8
-
-    def solve_x(index, _):
-        c = index // (my // tile)
-        base = lax.rem(index, my // tile) * tile
-        rows = [xlo[c, pl.ds(k * my + base, tile), :] for k in range(2)]
-        rows += [v[c, pl.ds(i * my + base, tile), :] for i in range(mx)]
-        rows += [xhi[c, pl.ds(k * my + base, tile), :] for k in range(2)]
-        pairs = [sides(lambda k, i=i: rows[i + 2 + k]) for i in range(mx)]
-        for s, out in ((0, fx), (1, sx)):
+    @pl.when(wall > 0)
+    def _():
+        y_up.wait_recv()
+
+    @pl.when(wall == 0)
+    def _():
+        ylo[...] = jnp.zeros_like(ylo)
+
+    @pl.when(wall < py - 1)
+    def _():
+        y_down.wait_recv()
+
+    @pl.when(wall == py - 1)
+    def _():
+        yhi[...] = jnp.zeros_like(yhi)
+
+    for copy in gy_copies:
+        copy.wait_recv()
+
+    def gathered(system, side):
+        return [[pick(wall, system.weights[side, q, way]) for way in range(2)] for q in range(py)]
+
+    low_y = [[pick(wall, -s.off * s.fix_low[:, k]) for k in range(3)] for s in sys_y]
+    high_y = [[pick(wall, -s.off * s.fix_high[:, k]) for k in range(3)] for s in sys_y]
+    outer_y = [[gathered(s, side) for side in range(2)] for s in sys_y]
+
+    wide = WIDE if mx % WIDE == 0 else 8
+
+    def solve_y(index, _):
+        c = index // (mx // wide)
+        base = lax.rem(index, mx // wide) * wide
+        part = pl.ds(base, wide)
+        rows = [ylo[c, k, part, :] for k in range(2)]
+        rows += [vt[c, y, part, :] for y in range(my)]
+        rows += [yhi[c, k, part, :] for k in range(2)]
+        pairs = [sides(lambda k, i=i: rows[i + 2 + k]) for i in range(my)]
+        for s, out in ((0, fy), (1, sy)):
             rhs = [pair[s] for pair in pairs]
+            ends = [
+                total([
+                    outer_y[s][side][q][way] * gyr[q, way, s, c, part, :]
+                    for q in range(py) for way in range(2)
+                ])
+                for side in range(2)
+            ]
             rhs[0] = rhs[0] + (
-                low_x[s][0] * rows[1] + low_x[s][1] * rows[0] + low_x[s][2] * rows[2]
+                low_y[s][0] * rows[1] + low_y[s][1] * rows[0] + low_y[s][2] * rows[2]
+                - sys_y[s].off * ends[0]
             )
-            rhs[mx - 1] = rhs[mx - 1] + (
-                high_x[s][0] * rows[mx + 2] + high_x[s][1] * rows[mx + 3] + high_x[s][2] * rows[mx + 1]
+            rhs[my - 1] = rhs[my - 1] + (
+                high_y[s][0] * rows[my + 2] + high_y[s][1] * rows[my + 3] + high_y[s][2] * rows[my + 1]
+                - sys_y[s].off * ends[1]
             )
-            for i, value in enumerate(sys_x[s].solve(rhs)):
-                out[c, pl.ds(i * my + base, tile), :] = value
-        return 0
-
-    lax.fori_loop(0, nc * (my // tile), solve_x, 0)
+            for i, value in enumerate(sys_y[s].solve(rhs)):
+                out[c, pl.ds(base * my + i, wide, stride=my), :] = value
+        return 0
+
+    lax.fori_loop(0, nc * (mx // wide), solve_y, 0)
 
     for copy, _ in first_round:
         copy.wait_recv()
@@ -325,84 +369,68 @@
         second_round.append(copy)
     ti[:, pl.ds(me * units, units)] = to[me]
 
-    @pl.when(wall > 0)
-    def _():
-        y_up.wait_recv()
-
-    @pl.when(wall == 0)
-    def _():
-        ylo[...] = jnp.zeros_like(ylo)
-
-    @pl.when(wall < py - 1)
-    def _():
-        y_down.wait_recv()
-
-    @pl.when(wall == py - 1)
-    def _():
-        yhi[...] = jnp.zeros_like(yhi)
-
-    for copy in gy_copies:
-        copy.wait_recv()
-
-    def gathered(system, side):
-        return [[pick(wall, system.weights[side, q, way]) for way in range(2)] for q in range(py)]
-
-    low_y = [[pick(wall, -s.off * s.fix_low[:, k]) for k in range(3)] for s in sys_y]
-    high_y = [[pick(wall, -s.off * s.fix_high[:, k]) for k in range(3)] for s in sys_y]
-    outer_y = [[gathered(s, side) for side in range(2)] for s in sys_y]
-
-    def solve_y(index, _):
-        c = index // (mx // 8)
-        base = lax.rem(index, mx // 8) * 8
-        part = pl.ds(base, 8)
-        rows = [ylo[k, c, part, :] for k in range(2)]
-        rows += [v[c, pl.ds(base * my + y, 8, stride=my), :] for y in range(my)]
-        rows += [yhi[k, c, part, :] for k in range(2)]
-        pairs = [sides(lambda k, i=i: rows[i + 2 + k]) for i in range(my)]
-        for s, out in ((0, fy), (1, sy)):
+    @pl.when(me > 0)
+    def _():
+        up.wait_recv()
+
+    @pl.when(me == 0)
+    def _():
+        xlo[...] = jnp.zeros_like(xlo)
+
+    @pl.when(me < px - 1)
+    def _():
+        down.wait_recv()
+
+    @pl.when(me == px - 1)
+    def _():
+        xhi[...] = jnp.zeros_like(xhi)
+
+    low_x = [[pick(me, -s.off * s.fix_low[:, k]) for k in range(3)] for s in sys_x]
+    high_x = [[pick(me, -s.off * s.fix_high[:, k]) for k in range(3)] for s in sys_x]
+    tile = 16 if my % 16 == 0 else 8
+
+    def solve_x(index, _):
+        c = index // (my // tile)
+        base = lax.rem(index, my // tile) * tile
+        rows = [xlo[c, pl.ds(k * my + base, tile), :] for k in range(2)]
+        rows += [v[c, pl.ds(i * my + base, tile), :] for i in range(mx)]
+        rows += [xhi[c, pl.ds(k * my + base, tile), :] for k in range(2)]
+        pairs = [sides(lambda k, i=i: rows[i + 2 + k]) for i in range(mx)]
+        for s, out in ((0, fx), (1, sx)):
             rhs = [pair[s] for pair in pairs]
-            ends = [
-                total([
-                    outer_y[s][side][q][way] * gyr[q, way, s, c, part, :]
-                    for q in range(py) for way in range(2)
-                ])
-                for side in range(2)
-            ]
             rhs[0] = rhs[0] + (
-                low_y[s][0] * rows[1] + low_y[s][1] * rows[0] + low_y[s][2] * rows[2]
-                - sys_y[s].off * ends[0]
+                low_x[s][0] * rows[1] + low_x[s][1] * rows[0] + low_x[s][2] * rows[2]
             )
-            rhs[my - 1] = rhs[my - 1] + (
-                high_y[s][0] * rows[my + 2] + high_y[s][1] * rows[my + 3] + high_y[s][2] * rows[my + 1]
-                - sys_y[s].off * ends[1]
+            rhs[mx - 1] = rhs[mx - 1] + (
+                high_x[s][0] * rows[mx + 2] + high_x[s][1] * rows[mx + 3] + high_x[s][2] * rows[mx + 1]
             )
-            for i, value in enumerate(sys_y[s].solve(rhs)):
-                out[c, pl.ds(base * my + i, 8, stride=my), :] = value
-        return 0
-
-    lax.fori_loop(0, nc * (mx // 8), solve_y, 0)
+            for i, value in enumerate(sys_x[s].solve(rhs)):
+                out[c, pl.ds(i * my + base, tile), :] = value
+        return 0
+
+    lax.fori_loop(0, nc * (my // tile), solve_x, 0)
 
     for copy in z_copies:
         copy.wait_recv()
 
+    for read in reads_cp:
+        read.wait()
+    slab = 4 * my
+
     def solve_z(index, _):
-        c = index // mx
-        part = pl.ds(lax.rem(index, mx) * my, my)
-        own, other = v[c, part, :], zo[c, part, :]
-        lane = lax.broadcasted_iota(jnp.int32, own.shape, 1)
-
-        def ahead(k):
-            return pltpu.roll(jnp.where(lane < k, other, own), nz - k, 1)
-
-        def back(k):
-            return pltpu.roll(jnp.where(lane >= nz - k, other, own), k, 1)
-
-        p1, m1, p2, m2, p3, m3 = ahead(1), back(1), ahead(2), back(2), ahead(3), back(3)
-        first = (45.0 / 60.0) * (p1 - m1) - (9.0 / 60.0) * (p2 - m2) + (1.0 / 60.0) * (p3 - m3)
-        second = (
-            (2.0 / 180.0) * (p3 + m3) - (27.0 / 180.0) * (p2 + m2)
-            + (270.0 / 180.0) * (p1 + m1) - (490.0 / 180.0) * own
-        )
+        c = index // (mx * my // slab)
+        part = pl.ds(lax.rem(index, mx * my // slab) * slab, slab)
+        own = v[c, part, :]
+        rest = jnp.concatenate([own, zo[c, part, :]], axis=1)
+        both_z = None
+        for step in range(3):
+            piece = rest.astype(jnp.bfloat16)
+            product = jnp.dot(piece, wz[...], preferred_element_type=jnp.float32)
+            both_z = product if both_z is None else both_z + product
+            if step < 2:
+                rest = rest - piece.astype(jnp.float32)
+        first = both_z[:, :nz] * (1.0 / 60.0)
+        second = both_z[:, nz:] * (1.0 / 180.0)
         moved = v[0, part, :] * fx[c, part, :] + v[1, part, :] * fy[c, part, :] + v[2, part, :] * first
         conv[c, part, :] = moved
         expl[c, part, :] = (
@@ -411,7 +439,7 @@
         )
         return 0
 
-    lax.fori_loop(0, nc * mx, solve_z, 0)
+    lax.fori_loop(0, nc * mx * my // slab, solve_z, 0)
 
     for copy in second_round:
         copy.wait_recv()
@@ -436,6 +464,7 @@
         low = high = None
         for i in range(my):
             row = yrow(expl, c, i)
+            et[c, i] = row
             low = right_w[i] * row if low is None else low + right_w[i] * row
             high = left_w[i] * row if high is None else high + left_w[i] * row
         gw[0, c] = low
@@ -451,14 +480,12 @@
     gwr[wall] = gw[...]
 
     def solve_w(index, _):
-        c = index // (mx // 8)
-        base = lax.rem(index, mx // 8) * 8
-        rows = [expl[c, pl.ds(base * my + y, 8, stride=my), :] for y in range(my)]
+        rows = [et[index, y] for y in range(my)]
         for i, value in enumerate(sys_w.solve(rows)):
-            upd[c, pl.ds(base * my + i, 8, stride=my), :] = value
-        return 0
-
-    lax.fori_loop(0, nc * (mx // 8), solve_w, 0)
+            et[index, i] = value
+        return 0
+
+    lax.fori_loop(0, nc, solve_w, 0)
     for copy in w_copies:
         copy.wait_recv()
     outer_w = [gathered(sys_w, side) for side in range(2)]
@@ -472,7 +499,7 @@
         ]
         for i in range(my):
             at = pl.ds(i, mx, stride=my)
-            upd[c, at, :] = upd[c, at, :] + (sys_w.low[i] * ends[0] + sys_w.high[i] * ends[1])
+            upd[c, at, :] = et[c, i] + (sys_w.low[i] * ends[0] + sys_w.high[i] * ends[1])
         return 0
 
     lax.fori_loop(0, nc, finish, 0)
@@ -516,28 +543,32 @@
         return pltpu.SemaphoreType.DMA((n,))
 
     whole = pl.BlockSpec(memory_space=pltpu.VMEM)
+    velocity = pltpu.with_memory_space_constraint(velocity.reshape(flat), pltpu.HBM)
+    conv_prev = pltpu.with_memory_space_constraint(conv_prev.reshape(flat), pltpu.HBM)
+    hbm = pl.BlockSpec(memory_space=pltpu.HBM)
     conv, upd = pl.pallas_call(
         functools.partial(kernel, (nc, mx, my, nz, px, py, units)),
         out_shape=[jax.ShapeDtypeStruct(flat, f32)] * 2,
-        in_specs=[whole, whole],
+        in_specs=[hbm, hbm],
         out_specs=[whole, whole],
         scratch_shapes=[
-            vmem(*flat),
+            vmem(*flat), vmem(*flat), dma(2 * nc),
+            pltpu.VMEM((2 * nz, 2 * nz), jnp.bfloat16), vmem(nc, my, mx, nz), vmem(*flat),
             vmem(nc, 2 * my, nz), vmem(nc, 2 * my, nz),
-            vmem(2, 2, nc, mx, nz), vmem(2, nc, mx, nz), vmem(2, nc, mx, nz),
+            vmem(nc, 2, mx, nz), vmem(nc, 2, mx, nz),
             vmem(2, px * units, 8, nz), vmem(px, 2, units, 8, nz),
             vmem(px, 2, units, 8, nz), vmem(2, px * units, 8, nz),
             vmem(2, 2, nc, mx, nz), vmem(py, 2, 2, nc, mx, nz),
             vmem(2, nc, mx, nz), vmem(py, 2, nc, mx, nz),
-            vmem(*flat), vmem(*flat), vmem(*flat), vmem(*flat), vmem(*flat),
+            vmem(*flat), vmem(*flat), vmem(*flat), vmem(*flat), vmem(*flat), vmem(nc, my, mx, nz),
             dma(px), dma(px), dma(px), dma(px), dma(2), dma(2), dma(2), dma(2),
             dma(py), dma(py), dma(py), dma(py), dma(nc), dma(nc),
         ],
         compiler_params=pltpu.CompilerParams(
             collective_id=0, has_side_effects=True, vmem_limit_bytes=32 * 1024 * 1024
         ),
-    )(velocity.reshape(flat), conv_prev.reshape(flat))
-    return conv.reshape(velocity.shape), upd.reshape(velocity.shape)
+    )(velocity, conv_prev)
+    return conv.reshape(nc, mx, my, nz), upd.reshape(nc, mx, my, nz)
 
 
 def solution(mesh):

time: 30.7 us -> 24.8 us (0.81)
  the two profiles are of different devices: /device:TPU:2 before, /device:TPU:0 now
where the time goes in v2:
time: 24.8 us; the launch traced here: 24.7 us
  Pallas kernels  22.3 us (90%)
  local copies, waits for them, and re-layouts  1.76 us (7%)
  between operations  0.64 us (3%)
    pallas_call x1, Pallas kernels, body(): pl.pallas_call(functools.partial(kernel, (nc, mx, my, nz, px, py, units))...  22.3 us
    unnamed x2, local copies, waits for them, and re-layouts  1.76 us

profile of v2, /device:TPU:0, one launch (start us, length us, event | category | flops | bytes accessed | tf_op | source)
XLA Modules:
  0.0 24.7 jit_solution(895020834460302116)
XLA Ops:
  0.6 22.3 %shard_map.41 = (f32[3,512,128]{2,1,0:T(8,128)S(1)}, f32[3,512,128]{2,1,0:T(8,128)S(1)}) custom-call(f32[3,512,128]{2,1,0:T(8,128)} %bitcast.6, f32[3,512,128]{2,1,0:T(8,128)} %bitcast.7), custom_call_target="tpu_custom_call" | custom-call | tf_op jit(solution)/shard_map/pallas_call | solution.py:549
  22.9 0.9 %copy.6 = f32[3,16,32,128]{3,2,1,0:T(8,128)} copy(f32[3,16,32,128]{3,2,1,0:T(8,128)S(1)} %bitcast.5) | data formatting | bytes 1572864
  23.8 0.9 %copy.7 = f32[3,16,32,128]{3,2,1,0:T(8,128)} copy(f32[3,16,32,128]{3,2,1,0:T(8,128)S(1)} %bitcast.4) | data formatting | bytes 1572864

commit v3 on v2

--- a/solution.py
+++ b/solution.py
@@ -415,20 +415,22 @@
 
     for read in reads_cp:
         read.wait()
-    slab = 4 * my
+    slab = mx * my
 
     def solve_z(index, _):
         c = index // (mx * my // slab)
         part = pl.ds(lax.rem(index, mx * my // slab) * slab, slab)
         own = v[c, part, :]
         rest = jnp.concatenate([own, zo[c, part, :]], axis=1)
-        both_z = None
+        pieces = []
         for step in range(3):
-            piece = rest.astype(jnp.bfloat16)
-            product = jnp.dot(piece, wz[...], preferred_element_type=jnp.float32)
-            both_z = product if both_z is None else both_z + product
+            pieces.append(rest.astype(jnp.bfloat16))
             if step < 2:
-                rest = rest - piece.astype(jnp.float32)
+                rest = rest - pieces[-1].astype(jnp.float32)
+        product = jnp.dot(
+            jnp.concatenate(pieces, axis=0), wz[...], preferred_element_type=jnp.float32
+        )
+        both_z = product[:slab] + (product[slab : 2 * slab] + product[2 * slab :])
         first = both_z[:, :nz] * (1.0 / 60.0)
         second = both_z[:, nz:] * (1.0 / 180.0)
         moved = v[0, part, :] * fx[c, part, :] + v[1, part, :] * fy[c, part, :] + v[2, part, :] * first
@@ -441,6 +443,10 @@
 
     lax.fori_loop(0, nc * mx * my // slab, solve_z, 0)
 
+    right_w = [pick(wall, sys_w.right[:, i]) for i in range(my)]
+    left_w = [pick(wall, sys_w.left[:, i]) for i in range(my)]
+
+    w_copies = []
     for copy in second_round:
         copy.wait_recv()
     for c in range(nc):
@@ -457,27 +463,22 @@
             conv[c, part, :] = conv[c, part, :] + moved
             expl[c, part, :] = expl[c, part, :] + (viscosity * bend - (time_step * gamma_now) * moved)
 
-    right_w = [pick(wall, sys_w.right[:, i]) for i in range(my)]
-    left_w = [pick(wall, sys_w.left[:, i]) for i in range(my)]
-
-    def sums_w(c, _):
         low = high = None
         for i in range(my):
             row = yrow(expl, c, i)
             et[c, i] = row
             low = right_w[i] * row if low is None else low + right_w[i] * row
             high = left_w[i] * row if high is None else high + left_w[i] * row
-        gw[0, c] = low
-        gw[1, c] = high
-        return 0
-
-    lax.fori_loop(0, nc, sums_w, 0)
-    w_copies = []
-    for d in range(1, py):
-        copy = remote(gw, gwr.at[wall], ws.at[d], wr.at[d], gy=gy_peer(d))
-        copy.start()
-        w_copies.append(copy)
-    gwr[wall] = gw[...]
+        gw[c, 0] = low
+        gw[c, 1] = high
+        copies = []
+        for d in range(1, py):
+            slot = (d - 1) * nc + c
+            copy = remote(gw.at[c], gwr.at[wall, c], ws.at[slot], wr.at[slot], gy=gy_peer(d))
+            copy.start()
+            copies.append(copy)
+        w_copies.append(copies)
+        gwr[wall, c] = gw[c]
 
     def solve_w(index, _):
         rows = [et[index, y] for y in range(my)]
@@ -486,27 +487,24 @@
         return 0
 
     lax.fori_loop(0, nc, solve_w, 0)
-    for copy in w_copies:
-        copy.wait_recv()
     outer_w = [gathered(sys_w, side) for side in range(2)]
 
-    def finish(c, _):
+    for c in range(nc):
+        for copy in w_copies[c]:
+            copy.wait_recv()
         ends = [
             total([
-                outer_w[side][q][way] * gwr[q, way, c] for q in range(py) for way in range(2)
+                outer_w[side][q][way] * gwr[q, c, way] for q in range(py) for way in range(2)
             ])
             for side in range(2)
         ]
         for i in range(my):
             at = pl.ds(i, mx, stride=my)
             upd[c, at, :] = et[c, i] + (sys_w.low[i] * ends[0] + sys_w.high[i] * ends[1])
-        return 0
-
-    lax.fori_loop(0, nc, finish, 0)
 
     for copy, _ in first_round:
         copy.wait_send()
-    for copy in second_round + z_copies + gy_copies + w_copies:
+    for copy in second_round + z_copies + gy_copies + sum(w_copies, []):
         copy.wait_send()
 
     @pl.when(me < px - 1)
@@ -559,10 +557,10 @@
             vmem(2, px * units, 8, nz), vmem(px, 2, units, 8, nz),
             vmem(px, 2, units, 8, nz), vmem(2, px * units, 8, nz),
             vmem(2, 2, nc, mx, nz), vmem(py, 2, 2, nc, mx, nz),
-            vmem(2, nc, mx, nz), vmem(py, 2, nc, mx, nz),
+            vmem(nc, 2, mx, nz), vmem(py, nc, 2, mx, nz),
             vmem(*flat), vmem(*flat), vmem(*flat), vmem(*flat), vmem(*flat), vmem(nc, my, mx, nz),
             dma(px), dma(px), dma(px), dma(px), dma(2), dma(2), dma(2), dma(2),
-            dma(py), dma(py), dma(py), dma(py), dma(nc), dma(nc),
+            dma(py), dma(py), dma(py * nc), dma(py * nc), dma(nc), dma(nc),
         ],
         compiler_params=pltpu.CompilerParams(
             collective_id=0, has_side_effects=True, vmem_limit_bytes=32 * 1024 * 1024

time: 24.8 us -> 24.1 us (0.972)
  Pallas kernels: 22.3 us -> 21.5 us
    pallas_call x1, Pallas kernels: 22.3 us -> 21.5 us  [body(): pl.pallas_call(functools.partial(kernel, (nc, mx, my, nz, px, py, units))...]
where the time goes in v3:
time: 24.1 us; the launch traced here: 23.9 us
  Pallas kernels  21.5 us (89%)
  local copies, waits for them, and re-layouts  1.76 us (7%)
  between operations  0.64 us (3%)
    pallas_call x1, Pallas kernels, body(): pl.pallas_call(functools.partial(kernel, (nc, mx, my, nz, px, py, units))...  21.5 us
    unnamed x2, local copies, waits for them, and re-layouts  1.76 us

profile of v3, /device:TPU:0, one launch (start us, length us, event | category | flops | bytes accessed | tf_op | source)
XLA Modules:
  0.0 23.9 jit_solution(6620400403807121309)
XLA Ops:
  0.6 21.5 %shard_map.41 = (f32[3,512,128]{2,1,0:T(8,128)S(1)}, f32[3,512,128]{2,1,0:T(8,128)S(1)}) custom-call(f32[3,512,128]{2,1,0:T(8,128)} %bitcast.6, f32[3,512,128]{2,1,0:T(8,128)} %bitcast.7), custom_call_target="tpu_custom_call" | custom-call | tf_op jit(solution)/shard_map/pallas_call | solution.py:547
  22.2 0.9 %copy.6 = f32[3,16,32,128]{3,2,1,0:T(8,128)} copy(f32[3,16,32,128]{3,2,1,0:T(8,128)S(1)} %bitcast.5) | data formatting | bytes 1572864
  23.1 0.9 %copy.7 = f32[3,16,32,128]{3,2,1,0:T(8,128)} copy(f32[3,16,32,128]{3,2,1,0:T(8,128)S(1)} %bitcast.4) | data formatting | bytes 1572864
